TPU v7x, 128 devices: a whole 4x4x4 slice. The times are simulated.
128 devices in a mesh: row: 16 (over x, z), col: 8 (over y, core).
Axes of the slice: x: 4, y: 4, z: 4, core: 2. Of those that a mesh axis runs over, the one named last changes fastest.
Arguments:
- qkv: bfloat16 [3, 1408, 32768], P(None, 'col', 'row'), may hold values from -12.1 to 12.1
- residual_in: bfloat16 [1408, 32768], P('col', 'row'), may hold values from -3 to 3
- out_weight: bfloat16 [1408, 1408], replicated, may hold values from -0.625 to 0.625
- merge_weight: bfloat16 [1408, 5632], P('col'), may hold values from -0.078125 to 0.078125
- merge_gain: float32 [1408], replicated, may hold values from 0.1 to 1.9
- image_groups: int32 [64], replicated, may hold values from 1 to 256, 8192 in all
- dest_row: int32 [8192], P('row'), may hold values from 0 to 8191, as said below
Outputs:
- layer_out: bfloat16 [1408, 32768], P('col', 'row')
- image_rows: bfloat16 [1408, 8192], P('col', 'row')
Inputs may be any that keep to these rules, and one draw needn't show every extreme that they name: dest_row is a permutation of 0 to 8191. Of the 512 entries held by each index of row, exactly 32 fall in each aligned block of 512 output rows.
All inputs are finite; a program needn't handle non-finite values.
Results may differ from a plain program's by a relative error of at most 0.0064.
Values may be sent and summed in bfloat16 or wider, within the bound.
A program may use at most 128 MiB of HBM per device.

v0:
```python
import math
import jax
import jax.numpy as jnp
from jax import lax
from jax.sharding import PartitionSpec as P

HEAD_DIM = 88


def with_halo(cells, sides, width):
    for axis, dim in sides:
        count = lax.axis_size(axis)
        ends = count - 1
        head = lax.slice_in_dim(cells, 0, width, axis=dim)
        tail = lax.slice_in_dim(cells, cells.shape[dim] - width, cells.shape[dim], axis=dim)
        cells = jnp.concatenate(
            [
                lax.ppermute(tail, axis, [(i, (i + 1) % count) for i in range(ends)]),
                cells,
                lax.ppermute(head, axis, [((i + 1) % count, i) for i in range(ends)]),
            ],
            axis=dim,
        )
    return cells


def image_labels(positions, image_ends, all_tokens):
    inside = (positions >= 0) & (positions < all_tokens)
    counted = jnp.sum((positions[:, None] >= image_ends[None, :]).astype(jnp.int32), axis=1)
    return jnp.where(inside, counted, -1)


def body(qkv, residual_in, out_weight, merge_weight, merge_gain, image_groups, dest_row):
    width_here = qkv.shape[1]
    tok_rows = qkv.shape[2]
    heads_here = width_here // HEAD_DIM
    full_width = out_weight.shape[0]
    reach_rows = tok_rows // 2
    block_rows = min(1024, tok_rows)
    block_count = tok_rows // block_rows
    window = block_rows + 2 * reach_rows
    row_count = lax.axis_size("row")
    row_id = lax.axis_index("row")
    col_id = lax.axis_index("col")
    all_tokens = tok_rows * row_count
    score_scale = 1.0 / math.sqrt(HEAD_DIM)
    image_ends = jnp.cumsum(image_groups) * 4
    extended = with_halo(qkv[1:], (("row", 2),), reach_rows)
    positions = (
        row_id * tok_rows - reach_rows + jnp.arange(tok_rows + 2 * reach_rows, dtype=jnp.int32)
    )
    labels = image_labels(positions, image_ends, all_tokens)

    def attend(block_id):
        first_row = block_id * block_rows
        queries = lax.dynamic_slice_in_dim(qkv[0], first_row, block_rows, 1).reshape(
            heads_here, HEAD_DIM, block_rows
        )
        key_block = lax.dynamic_slice_in_dim(extended[0], first_row, window, 1).reshape(
            heads_here, HEAD_DIM, window
        )
        value_block = lax.dynamic_slice_in_dim(extended[1], first_row, window, 1).reshape(
            heads_here, HEAD_DIM, window
        )
        query_labels = lax.dynamic_slice_in_dim(labels, first_row + reach_rows, block_rows, 0)
        key_labels = lax.dynamic_slice_in_dim(labels, first_row, window, 0)
        scores = (
            jnp.einsum("hdq,hdk->hqk", queries, key_block, preferred_element_type=jnp.float32)
            * score_scale
        )
        same_image = (query_labels[:, None] == key_labels[None, :])[None]
        scores = jnp.where(same_image, scores, -1e30)
        row_max = jnp.max(scores, axis=2, keepdims=True)
        exponent = jnp.exp(scores - row_max)
        totals = jnp.sum(exponent, axis=2)
        weights = exponent.astype(jnp.bfloat16)
        weighted = jnp.einsum(
            "hqk,hdk->hdq", weights, value_block, preferred_element_type=jnp.float32
        )
        weighted = weighted / totals[:, None, :]
        return weighted.astype(jnp.bfloat16).reshape(width_here, block_rows)

    attended = lax.map(attend, jnp.arange(block_count, dtype=jnp.int32))
    attended = jnp.transpose(attended, (1, 0, 2)).reshape(width_here, tok_rows)
    head_weight = lax.dynamic_slice_in_dim(out_weight, col_id * width_here, width_here, 0)
    partial_value = lax.dot_general(
        head_weight, attended, (((0,), (0,)), ((), ())), preferred_element_type=jnp.float32
    )
    projected = lax.psum_scatter(partial_value, "col", scatter_dimension=0, tiled=True)
    layer_out = (residual_in.astype(jnp.float32) + projected).astype(jnp.bfloat16)
    full_rows = lax.all_gather(layer_out, "col", axis=0, tiled=True)
    values32 = full_rows.astype(jnp.float32)
    centre = jnp.mean(values32, axis=0, keepdims=True)
    spread = jnp.mean(jnp.square(values32 - centre), axis=0, keepdims=True)
    normed = ((values32 - centre) * lax.rsqrt(spread + 1e-06) * merge_gain[:, None]).astype(
        jnp.bfloat16
    )
    group_rows = tok_rows // 4
    grouped = normed.reshape(full_width, group_rows, 4)
    weight_parts = merge_weight.reshape(width_here, 4, full_width)
    merged = jnp.einsum(
        "ojf,fgj->og", weight_parts, grouped, preferred_element_type=jnp.float32
    ).astype(jnp.bfloat16)
    empty_rows = jnp.zeros((width_here, group_rows), jnp.bfloat16)
    every_row, every_dest = (
        lax.all_gather(merged, "row", axis=1, tiled=True),
        lax.all_gather(dest_row, "row", axis=0, tiled=True),
    )
    slot_index = every_dest - row_id * group_rows
    slot_index = jnp.where((slot_index >= 0) & (slot_index < group_rows), slot_index, group_rows)
    image_rows = empty_rows.at[:, slot_index].set(every_row, mode="drop")
    return (layer_out, image_rows)


def solution(mesh):
    return jax.shard_map(
        body,
        mesh=mesh,
        in_specs=(P(None, "col", "row"), P("col", "row"), P(), P("col", None), P(), P(), P("row")),
        out_specs=(P("col", "row"), P("col", "row")),
        check_vma=False,
    )
```

profile of v0, /device:TPU:0, one launch (start us, length us, event | category | flops | bytes accessed | tf_op | source)
XLA Modules:
  0.0 381.6 jit_solution(7010875313808431647)
XLA Ops:
  7.2 2.4 fusion.44
  9.7 3.9 %collective-permute-start = (bf16[2,176,1024]{2,1,0:T(8,128)(2,1)}, bf16[2,176,1024]{2,1,0:T(8,128)(2,1)S(1)}, u32[]{:S(2)}, u32[]{:S(2)}) collective-permute-start(bf16[2,176,1024]{2,1,0:T(8,128)(2,1)} %get-tuple-element.106), channel_id=1, source_target_pairs={{0,8},{8,16},{16,24},{24,32},{32,40},{40,48},{48,56},{56,64},{64,7... | collective-permute-start | bytes 2162696 | tf_op jit(solution)/shard_map/ppermute | solution.py:18
  13.6 1.3 collective-permute-start.1
  15.0 0.1 copy.28
  15.1 0.1 reduce-window.8
  15.2 0.1 multiply_reduce_fusion
  15.3 0.2 convert_reduce_fusion.1
  15.5 13.8 %collective-permute-done = bf16[2,176,1024]{2,1,0:T(8,128)(2,1)S(1)} collective-permute-done((bf16[2,176,1024]{2,1,0:T(8,128)(2,1)}, bf16[2,176,1024]{2,1,0:T(8,128)(2,1)S(1)}, u32[]{:S(2)}, u32[]{:S(2)}) %collective-permute-start) | collective-permute-done | bytes 720928 | tf_op jit(solution)/shard_map/ppermute | solution.py:18
  29.3 4.1 %collective-permute-done.1 = bf16[2,176,1024]{2,1,0:T(8,128)(2,1)} collective-permute-done((bf16[2,176,1024]{2,1,0:T(8,128)(2,1)S(1)}, bf16[2,176,1024]{2,1,0:T(8,128)(2,1)}, u32[]{:S(2)}, u32[]{:S(2)}) %collective-permute-start.1) | collective-permute-done | bytes 720928 | tf_op jit(solution)/shard_map/ppermute | solution.py:20
  33.4 3.1 pad_maximum_fusion
  36.4 91.2 %while.12 = (s32[]{:T(128)}, bf16[2,176,1024]{2,1,0:T(8,128)(2,1)}, bf16[2,176,4096]{2,1,0:T(8,128)(2,1)}, s32[2]{0:T(128)S(1)}, s32[4096]{0:T(1024)S(1)}, /*ind...) while((s32[]{:T(128)}, bf16[2,176,1024]{2,1,0:T(8,128)(2,1)}, ...), condition=%wide.region_5.6_spmd, body=%wide.region_2.5_spmd.sunk | while | flops 2287300608 | bytes 108356392 | solution.py:83
  36.4 0.7 dynamic_slice.44
  37.8 2.0 broadcast_compare_fusion.2
  39.8 2.1 fusion.61
  41.9 1.6 constant_dynamic-slice_fusion.5
  43.6 1.2 slice.41
  44.8 12.6 %fusion.62 = (f32[2,1024]{1,0:T(2,128)S(1)}, f32[2,1024,3072]{2,1,0:T(8,128)}) fusion(pred[1024,3072]{1,0:T(8,128)(4,1)S(1)} %broadcast_compare_fusion.2, bf16[2,88,1024]{2,1,0:T(8,128)(2,1)S(1)} %bitcast.59, bf16[2,88,3072]{2,1,0:T(8,128)(2,1)} %bitcast.57), kind=kOutput, calls=%fused_computation.3.clone.1 | convolution fusion | flops 1126168576 | bytes 29761536 | tf_op jit(solution)/shard_map/while/body/eval_jaxpr/hdq,hdk->hqk/dot_general | solution.py:68
  57.4 12.0 %fusion.63 = f32[2,1024]{1,0:T(2,128)S(1)} fusion(f32[2,1024,3072]{2,1,0:T(8,128)} %get-tuple-element.155, f32[2,1024]{1,0:T(2,128)S(1)} %get-tuple-element.156, pred[1024,3072]{1,0:T(8,128)(4,1)S(1)} %broadcast_compare_fusion.2), kind=kLoop, calls=%fused_computation.4.clone.1 | loop fusion | flops 25163776 | bytes 28327936 | tf_op jit(solution)/shard_map/while/body/eval_jaxpr/reduce_sum | solution.py:75
  69.4 11.8 %fusion.64 = bf16[2,88,1024]{2,1,0:T(8,128)(2,1)S(1)} fusion(bf16[2,88,3072]{2,1,0:T(8,128)(2,1)S(1)} %bitcast.56, f32[2,1024,3072]{2,1,0:T(8,128)} %get-tuple-element.155, f32[2,1024]{1,0:T(2,128)S(1)} %get-tuple-element.156, pred[1024,3072]{1,0:T(8,128)(4,1)S(1)} %broadcast_compare_fusion.2, f32[2,1024]{1,0:T(2,128)S(1)} %fusion.63), kind=kOutput, calls=%fused_computation.10.clone.1 | convolution fusion | flops 1132822528 | bytes 29769728 | tf_op jit(solution)/shard_map/while/body/eval_jaxpr/hqk,hdk->hdq/dot_general | solution.py:77
  81.3 0.8 bitcast_dynamic-update-slice_fusion.2
  82.0 0.7 dynamic_slice.44
  83.4 2.0 broadcast_compare_fusion.2
  85.4 2.1 fusion.61
  87.5 1.6 constant_dynamic-slice_fusion.5
  89.2 1.2 slice.41
  90.4 12.6 %fusion.62 = (f32[2,1024]{1,0:T(2,128)S(1)}, f32[2,1024,3072]{2,1,0:T(8,128)}) fusion(pred[1024,3072]{1,0:T(8,128)(4,1)S(1)} %broadcast_compare_fusion.2, bf16[2,88,1024]{2,1,0:T(8,128)(2,1)S(1)} %bitcast.59, bf16[2,88,3072]{2,1,0:T(8,128)(2,1)} %bitcast.57), kind=kOutput, calls=%fused_computation.3.clone.1 | convolution fusion | flops 1126168576 | bytes 29761536 | tf_op jit(solution)/shard_map/while/body/eval_jaxpr/hdq,hdk->hqk/dot_general | solution.py:68
  103.0 12.0 %fusion.63 = f32[2,1024]{1,0:T(2,128)S(1)} fusion(f32[2,1024,3072]{2,1,0:T(8,128)} %get-tuple-element.155, f32[2,1024]{1,0:T(2,128)S(1)} %get-tuple-element.156, pred[1024,3072]{1,0:T(8,128)(4,1)S(1)} %broadcast_compare_fusion.2), kind=kLoop, calls=%fused_computation.4.clone.1 | loop fusion | flops 25163776 | bytes 28327936 | tf_op jit(solution)/shard_map/while/body/eval_jaxpr/reduce_sum | solution.py:75
  115.0 11.8 %fusion.64 = bf16[2,88,1024]{2,1,0:T(8,128)(2,1)S(1)} fusion(bf16[2,88,3072]{2,1,0:T(8,128)(2,1)S(1)} %bitcast.56, f32[2,1024,3072]{2,1,0:T(8,128)} %get-tuple-element.155, f32[2,1024]{1,0:T(2,128)S(1)} %get-tuple-element.156, pred[1024,3072]{1,0:T(8,128)(4,1)S(1)} %broadcast_compare_fusion.2, f32[2,1024]{1,0:T(2,128)S(1)} %fusion.63), kind=kOutput, calls=%fused_computation.10.clone.1 | convolution fusion | flops 1132822528 | bytes 29769728 | tf_op jit(solution)/shard_map/while/body/eval_jaxpr/hqk,hdk->hdq/dot_general | solution.py:77
  126.9 0.8 bitcast_dynamic-update-slice_fusion.2
  127.7 1.2 copy.36
  128.8 7.1 %fusion.38 = f32[1408,2048]{1,0:T(8,128)} fusion(bf16[176,2048]{1,0:T(8,128)(2,1)S(1)} %bitcast.61, bf16[1408,1408]{1,0:T(8,128)(2,1)} %param.11, s32[]{:T(128)S(6)} %select_n.41), kind=kOutput, calls=%fused_computation.34 | convolution fusion | flops 1015021568 | bytes 12750852 | tf_op jit(solution)/shard_map/dot_general | solution.py:86
  135.9 0.2 all-gather.4.cloned.1.call-start
  136.2 70.0 %reduce-scatter.2.cloned.1.call-done = f32[176,2048]{1,0:T(8,128)} async-done(((f32[1408,2048]{1,0:T(8,128)}), f32[176,2048]{1,0:T(8,128)}) %reduce-scatter.2.cloned.1.call-update) | async-done | bytes 1441808 | tf_op jit(solution)/shard_map/reduce_scatter | solution.py:89
  206.2 2.4 add_convert_fusion
  208.6 0.0 all-gather.6.cloned.1.call-start
  208.7 38.4 %all-gather.4.cloned.1.call-done = bf16[1408,2048]{1,0:T(8,128)(2,1)} async-done(((bf16[176,2048]{1,0:T(8,128)(2,1)}), bf16[1408,2048]{1,0:T(8,128)(2,1)}) %all-gather.4.cloned.1.call-update) | async-done | bytes 5767184 | tf_op jit(solution)/shard_map/all_gather | solution.py:91
  247.1 3.7 convert_reduce_fusion
  250.8 0.6 copy-done
  251.4 1.5 fusion.16
  253.0 4.3 %fusion.18 = bf16[1408,2048]{1,0:T(8,128)(2,1)} fusion(bf16[1408,2048]{1,0:T(8,128)(2,1)S(1)} %copy-done, f32[1408]{0:T(1024)S(1)} %copy-done.3, f32[2048]{0:T(1024)S(1)} %add_rsqrt_fusion, f32[2048]{0:T(1024)S(1)} %broadcast_multiply_fusion), kind=kLoop, calls=%fused_computation.23 | loop fusion | flops 14417920 | bytes 11556352 | tf_op jit(solution)/shard_map/convert_element_type | solution.py:95
  257.2 8.4 %copy.30 = bf16[1408,2048]{0,1:T(8,128)(2,1)} copy(bf16[1408,2048]{1,0:T(8,128)(2,1)} %fusion.18) | data formatting | bytes 11534336 | tf_op jit(solution)/shard_map/convert_element_type | solution.py:95
  265.6 10.6 %reshape.116 = bf16[1408,512,4]{0,2,1:T(4,128)(2,1)} reshape(bf16[1408,2048]{0,1:T(8,128)(2,1)} %copy.30) | data formatting | bytes 11534336 | tf_op jit(solution)/shard_map/reshape | solution.py:99
  276.2 5.4 %fusion.33 = bf16[176,512]{1,0:T(8,128)(2,1)} fusion(bf16[1408,512,4]{0,2,1:T(4,128)(2,1)} %reshape.116, bf16[22,4,8,1408]{3,2,1,0:T(8,128)(2,1)S(1)} %bitcast.67), kind=kOutput, calls=%fused_computation.32 | convolution fusion | flops 1015111680 | bytes 7929856 | tf_op jit(solution)/shard_map/ojf,fgj->og/dot_general | solution.py:101
  281.7 23.5 %all-gather = s32[16,1,512]{2,1,0:T(1,128)S(1)} all-gather(s32[1,1,512]{2,1,0:T(1,128)S(1)} %bitcast.65), channel_id=1, replica_groups=mesh['row'=16,'col'=8] {'row'}, dimensions={0}, use_global_device_ids=true | all-gather | bytes 34816 | tf_op jit(solution)/shard_map/all_gather | solution.py:107
  305.2 28.1 %all-gather.6.cloned.1.call-done = bf16[176,8192]{1,0:T(8,128)(2,1)} async-done(((bf16[176,512]{1,0:T(8,128)(2,1)}), bf16[176,8192]{1,0:T(8,128)(2,1)}) %all-gather.6.cloned.1.call-update) | async-done | bytes 2883600 | tf_op jit(solution)/shard_map/all_gather | solution.py:106
  333.3 5.8 %copy.33 = bf16[8192,176]{1,0:T(8,128)(2,1)} copy(bf16[8192,176]{0,1:T(8,128)(2,1)} %bitcast.60) | data formatting | bytes 5767168 | tf_op jit(solution)/shard_map/all_gather | solution.py:106
  339.1 35.2 %scatter_custom_fusion = bf16[176,512]{0,1:T(8,128)(2,1)S(1)} fusion(s32[8192]{0:T(1024)S(1)} %compare_select_fusion, bf16[8192,176]{1,0:T(8,128)(2,1)} %copy.33, bf16[]{:T(256)} %constant.97.clone.1), kind=kCustom, calls=%fused_computation.36 | custom fusion | bytes 180736 | tf_op jit(solution)/shard_map/scatter | solution.py:111
  374.3 0.8 copy.34
  (35 shorter events, 0.3 us)
Async XLA Ops:
  7.2 26.2 %slice-start = ((bf16[3,176,2048]{2,1,0:T(8,128)(2,1)}), bf16[2,176,2048]{2,1,0:T(8,128)(2,1)S(1)}, s32[]{:S(2)}) async-start(bf16[3,176,2048]{2,1,0:T(8,128)(2,1)} %param.9), calls=%async_computation.4 | async-start | bytes 2883584 | tf_op jit(solution)/shard_map/slice | solution.py:48
  7.2 7.8 %copy-start.5 = (s32[64]{0:T(128)S(1)}, s32[64]{0:T(128)}, u32[]{:S(2)}) copy-start(s32[64]{0:T(128)} %param.14) | copy-start | bytes 772
  7.2 199.0 %reduce-scatter.2.cloned.1.call-start = ((), (), s32[]{:S(2)}) async-start(), calls=%async_computation.1 | async-start | bytes 12976128 | tf_op jit(solution)/shard_map/reduce_scatter | solution.py:89
  9.7 19.6 %collective-permute-start = (bf16[2,176,1024]{2,1,0:T(8,128)(2,1)}, bf16[2,176,1024]{2,1,0:T(8,128)(2,1)S(1)}, u32[]{:S(2)}, u32[]{:S(2)}) collective-permute-start(bf16[2,176,1024]{2,1,0:T(8,128)(2,1)} %get-tuple-element.106), channel_id=1, source_target_pairs={{0,8},{8,16},{16,24},{24,32},{32,40},{40,48},{48,56},{56,64},{64,7... | collective-permute-start | bytes 2162696 | tf_op jit(solution)/shard_map/ppermute | solution.py:18
  13.6 19.7 %collective-permute-start.1 = (bf16[2,176,1024]{2,1,0:T(8,128)(2,1)S(1)}, bf16[2,176,1024]{2,1,0:T(8,128)(2,1)}, u32[]{:S(2)}, u32[]{:S(2)}) collective-permute-start(bf16[2,176,1024]{2,1,0:T(8,128)(2,1)S(1)} %get-tuple-element.107), channel_id=1, source_target_pairs={{8,0},{16,8},{24,16},{32,24},{40,32},{48,40},{56,48},{64,56},{72,6... | collective-permute-start | bytes 2162696 | tf_op jit(solution)/shard_map/ppermute | solution.py:20
  57.4 12.0 %copy-start.1 = (bf16[1,176,3072]{2,1,0:T(8,128)(2,1)S(1)}, bf16[1,176,3072]{2,1,0:T(8,128)(2,1)}, u32[]{:S(2)}) copy-start(bf16[1,176,3072]{2,1,0:T(8,128)(2,1)} %get-tuple-element.153) | copy-start | bytes 3244036 | tf_op jit(solution)/shard_map/while
  103.0 12.0 %copy-start.1 = (bf16[1,176,3072]{2,1,0:T(8,128)(2,1)S(1)}, bf16[1,176,3072]{2,1,0:T(8,128)(2,1)}, u32[]{:S(2)}) copy-start(bf16[1,176,3072]{2,1,0:T(8,128)(2,1)} %get-tuple-element.153) | copy-start | bytes 3244036 | tf_op jit(solution)/shard_map/while
  135.9 70.3 %copy-start.2 = (bf16[176,2048]{1,0:T(8,128)(2,1)S(1)}, bf16[176,2048]{1,0:T(8,128)(2,1)}, u32[]{:S(2)}) copy-start(bf16[176,2048]{1,0:T(8,128)(2,1)} %param.10) | copy-start | bytes 2162692
  135.9 111.1 %all-gather.4.cloned.1.call-start = ((), (), s32[]{:S(2)}) async-start(), calls=%async_computation.2 | async-start | bytes 6488064 | tf_op jit(solution)/shard_map/all_gather | solution.py:91
  208.6 44.3 %copy-start.3 = (f32[1408]{0:T(1024)S(1)}, f32[1408]{0:T(1024)}, u32[]{:S(2)}) copy-start(f32[1408]{0:T(1024)} %param.13) | copy-start | bytes 16900
  208.6 124.7 %all-gather.6.cloned.1.call-start = ((), (), s32[]{:S(2)}) async-start(), calls=%async_computation.3 | async-start | bytes 3063808 | tf_op jit(solution)/shard_map/all_gather | solution.py:106
  247.1 4.3 %copy-start = (bf16[1408,2048]{1,0:T(8,128)(2,1)S(1)}, bf16[1408,2048]{1,0:T(8,128)(2,1)}, u32[]{:S(2)}) copy-start(bf16[1408,2048]{1,0:T(8,128)(2,1)} %all-gather.4.cloned.1.call-done) | copy-start | bytes 17301508
  265.6 10.7 %copy-start.6 = (bf16[176,5632]{1,0:T(8,128)(2,1)S(1)}, bf16[176,5632]{1,0:T(8,128)(2,1)}, u32[]{:S(2)}) copy-start(bf16[176,5632]{1,0:T(8,128)(2,1)} %param.12) | copy-start | bytes 5947396
  276.2 5.4 %copy-start.4 = (s32[512]{0:T(512)S(1)}, s32[512]{0:T(512)}, u32[]{:S(2)}) copy-start(s32[512]{0:T(512)} %param.15) | copy-start | bytes 6148
Sparse Core Ops, SparseCore 0:
  136.1 70.0 reduce-scatter.1
  208.7 38.2 all-gather.3
  281.8 51.4 all-gather.5
where the time goes:
time: 383 us; the launch traced here: 382 us
  waiting for transfers between devices  154 us (40%)
  local copies, waits for them, and re-layouts  77.9 us (20%)
  matrix products  61.4 us (16%)
  other arithmetic  43.4 us (11%)
  blocking collectives  23.5 us (6%)
  between operations  13.9 us (4%)
  starting transfers between devices  5.53 us (1%)
    reduce_scatter x1, waiting for transfers between devices, body(): lax.psum_scatter(partial_value, 'col', scatter_dimension=0, tiled=True)  70 us
    all_gather x1, waiting for transfers between devices, body(): full_rows = lax.all_gather(layer_out, 'col', axis=0, tiled=True)  38.4 us
    scatter x1, local copies, waits for them, and re-layouts, body(): image_rows = empty_rows.at[:, slot_index].set(every_row, mode='drop')  35.2 us
    all_gather x1, waiting for transfers between devices, body(): lax.all_gather(merged, 'row', axis=1, tiled=True)  28.1 us
    dot_general x2, matrix products, attend(): jnp.einsum('hdq,hdk->hqk', queries, key_block, preferred_element_type=jnp...  25.3 us
    reduce_sum x2, other arithmetic, attend(): totals = jnp.sum(exponent, axis=2)  24 us
    dot_general x2, matrix products, attend(): jnp.einsum('hqk,hdk->hdq', weights, value_block, preferred_element_type=j...  23.7 us
    all_gather x1, blocking collectives, body(): lax.all_gather(dest_row, 'row', axis=0, tiled=True)  23.5 us
  transfers between devices with their start and end apart: 5, of which 5 were waited for; matrix products, arithmetic and copies ran while one was open for 0% of the time, Pallas kernels for 0%

commit v1 on v0

--- a/solution.py
+++ b/solution.py
@@ -5,6 +5,27 @@
 from jax.sharding import PartitionSpec as P
 
 HEAD_DIM = 88
+
+
+def ring_gather(value, axis, dim):
+    size, position, span = (lax.axis_size(axis), lax.axis_index(axis), value.shape[dim])
+    right = [(i, (i + 1) % size) for i in range(size)]
+    backward = [(i, (i - 1) % size) for i in range(size)]
+    out = jnp.zeros((*value.shape[:dim], size * span, *value.shape[dim + 1 :]), value.dtype)
+    out = lax.dynamic_update_slice_in_dim(out, value, position * span, axis=dim)
+    from_left = from_right = value
+    middle = size // 2
+    for step in range(1, middle + 1):
+        from_left = lax.ppermute(from_left, axis, right)
+        out = lax.dynamic_update_slice_in_dim(
+            out, from_left, (position - step) % size * span, axis=dim
+        )
+        if step < size - middle:
+            from_right = lax.ppermute(from_right, axis, backward)
+            out = lax.dynamic_update_slice_in_dim(
+                out, from_right, (position + step) % size * span, axis=dim
+            )
+    return out
 
 
 def with_halo(cells, sides, width):
@@ -88,7 +109,7 @@
     )
     projected = lax.psum_scatter(partial_value, "col", scatter_dimension=0, tiled=True)
     layer_out = (residual_in.astype(jnp.float32) + projected).astype(jnp.bfloat16)
-    full_rows = lax.all_gather(layer_out, "col", axis=0, tiled=True)
+    full_rows = ring_gather(layer_out, "col", 0)
     values32 = full_rows.astype(jnp.float32)
     centre = jnp.mean(values32, axis=0, keepdims=True)
     spread = jnp.mean(jnp.square(values32 - centre), axis=0, keepdims=True)

time: 383 us -> 479 us (1.25)
  local copies, waits for them, and re-layouts: 77.9 us -> 174 us
  waiting for transfers between devices: 154 us -> 143 us
  starting transfers between devices: 5.53 us -> 15.8 us
    dynamic_update_slice x0 -> x8, local copies, waits for them, and re-layouts: none -> 89.2 us  [the longest x4 44.7 us: ring_gather(): lax.dynamic_update_slice_in_dim(out, from_left, (position - step) % size...]
    all_gather x1 -> x0, waiting for transfers between devices: 38.4 us -> none  [body(): full_rows = lax.all_gather(layer_out, 'col', axis=0, tiled=True)]
    ppermute x0 -> x7, waiting for transfers between devices: none -> 26.9 us  [the longest x4 26.9 us: ring_gather(): from_left = lax.ppermute(from_left, axis, right)]
    ppermute x1, waiting for transfers between devices: 13.8 us -> 0.97 us  [with_halo(): lax.ppermute(tail, axis, [(i, (i + 1) % count) for i in range(ends)])]
    ppermute x1, waiting for transfers between devices: 4.09 us -> 13 us  [with_halo(): lax.ppermute(head, axis, [((i + 1) % count, i) for i in range(ends)])]
    ppermute x0 -> x7, starting transfers between devices: none -> 8.86 us  [the longest x3 8.84 us: ring_gather(): from_right = lax.ppermute(from_right, axis, backward)]
    ppermute x0 -> x7, local copies, waits for them, and re-layouts: none -> 8.09 us  [the longest x4 4.75 us: ring_gather(): from_left = lax.ppermute(from_left, axis, right)]
    convert_element_type x1, local copies, waits for them, and re-layouts: 8.37 us -> 0.51 us  [body(): (residual_in.astype(jnp.float32) + projected).astype(jnp.bfloat16)]
  transfers between devices with their start and end apart: 5 -> 11, of which waited for: 5 -> 7; matrix products, arithmetic and copies ran while one was open for 0% -> 19% of each run, Pallas kernels for 0% -> 0%
where the time goes in v1:
time: 479 us; the launch traced here: 475 us
  local copies, waits for them, and re-layouts  174 us (36%)
  waiting for transfers between devices  143 us (30%)
  matrix products  61.4 us (13%)
  other arithmetic  42.2 us (9%)
  blocking collectives  23.7 us (5%)
  starting transfers between devices  15.8 us (3%)
  between operations  14.4 us (3%)
    reduce_scatter x1, waiting for transfers between devices, body(): lax.psum_scatter(partial_value, 'col', scatter_dimension=0, tiled=True)  72.8 us
    dynamic_update_slice x4, local copies, waits for them, and re-layouts, ring_gather(): lax.dynamic_update_slice_in_dim(out, from_left, (position - step) % size...  44.7 us
    scatter x1, local copies, waits for them, and re-layouts, body(): image_rows = empty_rows.at[:, slot_index].set(every_row, mode='drop')  35.2 us
    dynamic_update_slice x3, local copies, waits for them, and re-layouts, ring_gather(): lax.dynamic_update_slice_in_dim(out, from_right, (position + step) % size...  34.3 us
    all_gather x1, waiting for transfers between devices, body(): lax.all_gather(merged, 'row', axis=1, tiled=True)  29 us
    ppermute x4, waiting for transfers between devices, ring_gather(): from_left = lax.ppermute(from_left, axis, right)  26.9 us
    dot_general x2, matrix products, attend(): jnp.einsum('hdq,hdk->hqk', queries, key_block, preferred_element_type=jnp...  25.2 us
    reduce_sum x2, other arithmetic, attend(): totals = jnp.sum(exponent, axis=2)  24 us
  transfers between devices with their start and end apart: 11, of which 7 were waited for; matrix products, arithmetic and copies ran while one was open for 19% of the time, Pallas kernels for 0%

profile of v1, /device:TPU:0, one launch (start us, length us, event | category | flops | bytes accessed | tf_op | source)
XLA Modules:
  0.0 475.1 jit_solution(13865369379133073010)
XLA Ops:
  7.2 2.5 fusion.44
  11.0 5.4 %collective-permute-start = (bf16[2,176,1024]{2,1,0:T(8,128)(2,1)S(1)}, bf16[2,176,1024]{2,1,0:T(8,128)(2,1)}, u32[]{:S(2)}, u32[]{:S(2)}) collective-permute-start(bf16[2,176,1024]{2,1,0:T(8,128)(2,1)S(1)} %get-tuple-element.106), channel_id=1, source_target_pairs={{0,8},{8,16},{16,24},{24,32},{32,40},{40,48},{48,56},{56,64},{64,7... | collective-permute-start | bytes 2162696 | tf_op jit(solution)/shard_map/ppermute | solution.py:39
  17.0 13.0 %collective-permute-done.1 = bf16[2,176,1024]{2,1,0:T(8,128)(2,1)S(1)} collective-permute-done((bf16[2,176,1024]{2,1,0:T(8,128)(2,1)}, bf16[2,176,1024]{2,1,0:T(8,128)(2,1)S(1)}, u32[]{:S(2)}, u32[]{:S(2)}) %collective-permute-start.1) | collective-permute-done | bytes 720928 | tf_op jit(solution)/shard_map/ppermute | solution.py:41
  30.9 3.0 pad_maximum_fusion
  34.0 94.3 %while.12 = (s32[]{:T(128)}, bf16[2,176,1024]{2,1,0:T(8,128)(2,1)}, bf16[2,176,4096]{2,1,0:T(8,128)(2,1)}, s32[2]{0:T(128)S(1)}, s32[4096]{0:T(1024)S(1)}, /*ind...) while((s32[]{:T(128)}, bf16[2,176,1024]{2,1,0:T(8,128)(2,1)}, ...), condition=%wide.region_5.6_spmd, body=%wide.region_2.5_spmd.sunk | while | flops 2287300608 | bytes 108355888 | solution.py:104
  34.0 2.0 fusion.61
  37.2 1.6 constant_dynamic-slice_fusion.5
  38.8 2.0 broadcast_compare_fusion.2
  40.8 2.0 slice.41
  43.9 12.6 %fusion.62 = (f32[2,1024]{1,0:T(2,128)S(1)}, f32[2,1024,3072]{2,1,0:T(8,128)}) fusion(pred[1024,3072]{1,0:T(8,128)(4,1)S(1)} %broadcast_compare_fusion.2, bf16[2,88,1024]{2,1,0:T(8,128)(2,1)S(1)} %bitcast.59, bf16[2,88,3072]{2,1,0:T(8,128)(2,1)} %bitcast.57), kind=kOutput, calls=%fused_computation.3.clone.1 | convolution fusion | flops 1126168576 | bytes 29761536 | tf_op jit(solution)/shard_map/while/body/eval_jaxpr/hdq,hdk->hqk/dot_general | solution.py:89
  56.5 12.0 %fusion.63 = f32[2,1024]{1,0:T(2,128)S(1)} fusion(f32[2,1024,3072]{2,1,0:T(8,128)} %get-tuple-element.155, f32[2,1024]{1,0:T(2,128)S(1)} %get-tuple-element.156, pred[1024,3072]{1,0:T(8,128)(4,1)S(1)} %broadcast_compare_fusion.2), kind=kLoop, calls=%fused_computation.4.clone.1 | loop fusion | flops 25163776 | bytes 28327936 | tf_op jit(solution)/shard_map/while/body/eval_jaxpr/reduce_sum | solution.py:96
  68.5 11.8 %fusion.64 = bf16[2,88,1024]{2,1,0:T(8,128)(2,1)S(1)} fusion(bf16[2,88,3072]{2,1,0:T(8,128)(2,1)S(1)} %bitcast.56, f32[2,1024,3072]{2,1,0:T(8,128)} %get-tuple-element.155, f32[2,1024]{1,0:T(2,128)S(1)} %get-tuple-element.156, pred[1024,3072]{1,0:T(8,128)(4,1)S(1)} %broadcast_compare_fusion.2, f32[2,1024]{1,0:T(2,128)S(1)} %fusion.63), kind=kOutput, calls=%fused_computation.10.clone.1 | convolution fusion | flops 1132822528 | bytes 29769728 | tf_op jit(solution)/shard_map/while/body/eval_jaxpr/hqk,hdk->hdq/dot_general | solution.py:98
  81.1 2.0 fusion.61
  84.3 1.6 constant_dynamic-slice_fusion.5
  86.0 2.0 broadcast_compare_fusion.2
  87.9 2.0 slice.41
  91.0 12.6 %fusion.62 = (f32[2,1024]{1,0:T(2,128)S(1)}, f32[2,1024,3072]{2,1,0:T(8,128)}) fusion(pred[1024,3072]{1,0:T(8,128)(4,1)S(1)} %broadcast_compare_fusion.2, bf16[2,88,1024]{2,1,0:T(8,128)(2,1)S(1)} %bitcast.59, bf16[2,88,3072]{2,1,0:T(8,128)(2,1)} %bitcast.57), kind=kOutput, calls=%fused_computation.3.clone.1 | convolution fusion | flops 1126168576 | bytes 29761536 | tf_op jit(solution)/shard_map/while/body/eval_jaxpr/hdq,hdk->hqk/dot_general | solution.py:89
  103.6 12.0 %fusion.63 = f32[2,1024]{1,0:T(2,128)S(1)} fusion(f32[2,1024,3072]{2,1,0:T(8,128)} %get-tuple-element.155, f32[2,1024]{1,0:T(2,128)S(1)} %get-tuple-element.156, pred[1024,3072]{1,0:T(8,128)(4,1)S(1)} %broadcast_compare_fusion.2), kind=kLoop, calls=%fused_computation.4.clone.1 | loop fusion | flops 25163776 | bytes 28327936 | tf_op jit(solution)/shard_map/while/body/eval_jaxpr/reduce_sum | solution.py:96
  115.6 11.8 %fusion.64 = bf16[2,88,1024]{2,1,0:T(8,128)(2,1)S(1)} fusion(bf16[2,88,3072]{2,1,0:T(8,128)(2,1)S(1)} %bitcast.56, f32[2,1024,3072]{2,1,0:T(8,128)} %get-tuple-element.155, f32[2,1024]{1,0:T(2,128)S(1)} %get-tuple-element.156, pred[1024,3072]{1,0:T(8,128)(4,1)S(1)} %broadcast_compare_fusion.2, f32[2,1024]{1,0:T(2,128)S(1)} %fusion.63), kind=kOutput, calls=%fused_computation.10.clone.1 | convolution fusion | flops 1132822528 | bytes 29769728 | tf_op jit(solution)/shard_map/while/body/eval_jaxpr/hqk,hdk->hdq/dot_general | solution.py:98
  129.4 7.1 %fusion.38 = f32[1408,2048]{1,0:T(8,128)} fusion(bf16[176,2048]{1,0:T(8,128)(2,1)S(1)} %bitcast.61, bf16[1408,1408]{1,0:T(8,128)(2,1)} %param.11, s32[]{:T(128)S(6)} %select_n.94), kind=kOutput, calls=%fused_computation.34 | convolution fusion | flops 1015021568 | bytes 12750852 | tf_op jit(solution)/shard_map/dot_general | solution.py:107
  136.8 72.8 %reduce-scatter.2.cloned.1.call-done = f32[176,2048]{1,0:T(8,128)} async-done(((f32[1408,2048]{1,0:T(8,128)}), f32[176,2048]{1,0:T(8,128)}) %reduce-scatter.2.cloned.1.call-update) | async-done | bytes 1441808 | tf_op jit(solution)/shard_map/reduce_scatter | solution.py:110
  209.5 1.5 add_convert_fusion
  211.1 2.9 collective-permute-start.3
  214.1 9.0 %collective-permute-done.2 = bf16[176,2048]{1,0:T(8,128)(2,1)S(1)} collective-permute-done((bf16[176,2048]{1,0:T(8,128)(2,1)S(1)}, bf16[176,2048]{1,0:T(8,128)(2,1)S(1)}, u32[]{:S(2)}, u32[]{:S(2)}) %collective-permute-start.2) | collective-permute-done | bytes 720928 | tf_op jit(solution)/shard_map/ppermute | solution.py:19
  223.0 2.9 collective-permute-start.5
  226.0 9.0 %collective-permute-done.4 = bf16[176,2048]{1,0:T(8,128)(2,1)S(1)} collective-permute-done((bf16[176,2048]{1,0:T(8,128)(2,1)S(1)}, bf16[176,2048]{1,0:T(8,128)(2,1)S(1)}, u32[]{:S(2)}, u32[]{:S(2)}) %collective-permute-start.4) | collective-permute-done | bytes 720928 | tf_op jit(solution)/shard_map/ppermute | solution.py:19
  235.0 3.0 collective-permute-start.7
  237.9 9.0 %collective-permute-done.6 = bf16[176,2048]{1,0:T(8,128)(2,1)S(1)} collective-permute-done((bf16[176,2048]{1,0:T(8,128)(2,1)S(1)}, bf16[176,2048]{1,0:T(8,128)(2,1)S(1)}, u32[]{:S(2)}, u32[]{:S(2)}) %collective-permute-start.6) | collective-permute-done | bytes 720928 | tf_op jit(solution)/shard_map/ppermute | solution.py:19
  247.5 2.9 broadcast_in_dim.58
  250.4 10.2 %dynamic_update_slice.31 = bf16[1408,2048]{0,1:T(8,128)(2,1)} dynamic-update-slice(bf16[1408,2048]{0,1:T(8,128)(2,1)} %broadcast_in_dim.58, bf16[176,2048]{0,1:T(8,128)(2,1)S(1)} %copy.43, s32[]{:T(128)S(6)} %select_n.94, s32[]{:T(128)} %constant.138.clone.1) | dynamic-update-slice | bytes 1441796 | tf_op jit(solution)/shard_map/dynamic_update_slice | solution.py:15
  262.1 10.7 %dynamic_update_slice.32 = bf16[1408,2048]{0,1:T(8,128)(2,1)} dynamic-update-slice(bf16[1408,2048]{0,1:T(8,128)(2,1)} %dynamic_update_slice.31, bf16[176,2048]{0,1:T(8,128)(2,1)S(1)} %copy.44, s32[]{:T(128)S(6)} %select_n.99, s32[]{:T(128)} %constant.138.clone.1) | dynamic-update-slice | bytes 1441796 | tf_op jit(solution)/shard_map/dynamic_update_slice | solution.py:20
  274.2 11.5 %dynamic_update_slice.33 = bf16[1408,2048]{0,1:T(8,128)(2,1)} dynamic-update-slice(bf16[1408,2048]{0,1:T(8,128)(2,1)} %dynamic_update_slice.32, bf16[176,2048]{0,1:T(8,128)(2,1)S(1)} %copy.45, s32[]{:T(128)S(6)} %select_n.101, s32[]{:T(128)} %constant.138.clone.1) | dynamic-update-slice | bytes 1441796 | tf_op jit(solution)/shard_map/dynamic_update_slice | solution.py:25
  287.1 11.2 %dynamic_update_slice.34 = bf16[1408,2048]{0,1:T(8,128)(2,1)} dynamic-update-slice(bf16[1408,2048]{0,1:T(8,128)(2,1)} %dynamic_update_slice.33, bf16[176,2048]{0,1:T(8,128)(2,1)S(1)} %copy.46, s32[]{:T(128)S(6)} %select_n.103, s32[]{:T(128)} %constant.138.clone.1) | dynamic-update-slice | bytes 1441796 | tf_op jit(solution)/shard_map/dynamic_update_slice | solution.py:20
  298.8 11.4 %dynamic_update_slice.35 = bf16[1408,2048]{0,1:T(8,128)(2,1)} dynamic-update-slice(bf16[1408,2048]{0,1:T(8,128)(2,1)} %dynamic_update_slice.34, bf16[176,2048]{0,1:T(8,128)(2,1)S(1)} %copy.47, s32[]{:T(128)S(6)} %select_n.105, s32[]{:T(128)} %constant.138.clone.1) | dynamic-update-slice | bytes 1441796 | tf_op jit(solution)/shard_map/dynamic_update_slice | solution.py:25
  310.7 11.4 %dynamic_update_slice.36 = bf16[1408,2048]{0,1:T(8,128)(2,1)} dynamic-update-slice(bf16[1408,2048]{0,1:T(8,128)(2,1)} %dynamic_update_slice.35, bf16[176,2048]{0,1:T(8,128)(2,1)S(1)} %copy.48, s32[]{:T(128)S(6)} %select_n.107, s32[]{:T(128)} %constant.138.clone.1) | dynamic-update-slice | bytes 1441796 | tf_op jit(solution)/shard_map/dynamic_update_slice | solution.py:20
  322.1 1.4 copy.49
  323.6 11.4 %dynamic_update_slice.37 = bf16[1408,2048]{0,1:T(8,128)(2,1)} dynamic-update-slice(bf16[1408,2048]{0,1:T(8,128)(2,1)} %dynamic_update_slice.36, bf16[176,2048]{0,1:T(8,128)(2,1)S(1)} %copy.49, s32[]{:T(128)S(6)} %select_n.109, s32[]{:T(128)} %constant.138.clone.1) | dynamic-update-slice | bytes 1441796 | tf_op jit(solution)/shard_map/dynamic_update_slice | solution.py:25
  335.0 1.4 copy.50
  336.4 11.4 %dynamic_update_slice.38 = bf16[1408,2048]{0,1:T(8,128)(2,1)} dynamic-update-slice(bf16[1408,2048]{0,1:T(8,128)(2,1)} %dynamic_update_slice.37, bf16[176,2048]{0,1:T(8,128)(2,1)S(1)} %copy.50, s32[]{:T(128)S(6)} %select_n.111, s32[]{:T(128)} %constant.138.clone.1) | dynamic-update-slice | bytes 1441796 | tf_op jit(solution)/shard_map/dynamic_update_slice | solution.py:20
  347.8 3.6 convert_reduce_fusion
  352.1 1.6 fusion.16
  353.8 4.0 fusion.18
  357.8 10.6 %reshape.116 = bf16[1408,512,4]{0,2,1:T(4,128)(2,1)} reshape(bf16[1408,2048]{0,1:T(8,128)(2,1)} %fusion.18) | data formatting | bytes 11534336 | tf_op jit(solution)/shard_map/reshape | solution.py:120
  368.4 5.4 %fusion.33 = bf16[176,512]{1,0:T(8,128)(2,1)} fusion(bf16[1408,512,4]{0,2,1:T(4,128)(2,1)} %reshape.116, bf16[22,4,8,1408]{3,2,1,0:T(8,128)(2,1)S(1)} %bitcast.67), kind=kOutput, calls=%fused_computation.32 | convolution fusion | flops 1015111680 | bytes 7929856 | tf_op jit(solution)/shard_map/ojf,fgj->og/dot_general | solution.py:122
  373.9 23.7 %all-gather = s32[16,1,512]{2,1,0:T(1,128)S(1)} all-gather(s32[1,1,512]{2,1,0:T(1,128)S(1)} %bitcast.65), channel_id=1, replica_groups=mesh['row'=16,'col'=8] {'row'}, dimensions={0}, use_global_device_ids=true | all-gather | bytes 34816 | tf_op jit(solution)/shard_map/all_gather | solution.py:128
  397.6 29.0 %all-gather.3.cloned.1.call-done = bf16[176,8192]{1,0:T(8,128)(2,1)} async-done(((bf16[176,512]{1,0:T(8,128)(2,1)}), bf16[176,8192]{1,0:T(8,128)(2,1)}) %all-gather.3.cloned.1.call-update) | async-done | bytes 2883600 | tf_op jit(solution)/shard_map/all_gather | solution.py:127
  426.5 5.8 %copy.53 = bf16[8192,176]{1,0:T(8,128)(2,1)} copy(bf16[8192,176]{0,1:T(8,128)(2,1)} %bitcast.60) | data formatting | bytes 5767168 | tf_op jit(solution)/shard_map/all_gather | solution.py:127
  432.3 35.2 %scatter_custom_fusion = bf16[176,512]{0,1:T(8,128)(2,1)S(1)} fusion(s32[8192]{0:T(1024)S(1)} %compare_select_fusion, bf16[8192,176]{1,0:T(8,128)(2,1)} %copy.53, bf16[]{:T(256)} %constant.140.clone.1), kind=kCustom, calls=%fused_computation.36 | custom fusion | bytes 180736 | tf_op jit(solution)/shard_map/scatter | solution.py:132
  (70 shorter events, 16.4 us)
Async XLA Ops:
  7.2 23.8 %slice-start = ((bf16[3,176,2048]{2,1,0:T(8,128)(2,1)}), bf16[2,176,2048]{2,1,0:T(8,128)(2,1)S(1)}, s32[]{:S(2)}) async-start(bf16[3,176,2048]{2,1,0:T(8,128)(2,1)} %param.9), calls=%async_computation.3 | async-start | bytes 2883584 | tf_op jit(solution)/shard_map/slice | solution.py:69
  7.2 9.2 %copy-start.9 = (s32[64]{0:T(128)S(1)}, s32[64]{0:T(128)}, u32[]{:S(2)}) copy-start(s32[64]{0:T(128)} %param.14) | copy-start | bytes 772
  7.2 202.4 %reduce-scatter.2.cloned.1.call-start = ((), (), s32[]{:S(2)}) async-start(), calls=%async_computation.1 | async-start | bytes 12976128 | tf_op jit(solution)/shard_map/reduce_scatter | solution.py:110
  9.7 20.2 %collective-permute-start.1 = (bf16[2,176,1024]{2,1,0:T(8,128)(2,1)}, bf16[2,176,1024]{2,1,0:T(8,128)(2,1)S(1)}, u32[]{:S(2)}, u32[]{:S(2)}) collective-permute-start(bf16[2,176,1024]{2,1,0:T(8,128)(2,1)} %get-tuple-element.107), channel_id=1, source_target_pairs={{8,0},{16,8},{24,16},{32,24},{40,32},{48,40},{56,48},{64,56},{72,6... | collective-permute-start | bytes 2162696 | tf_op jit(solution)/shard_map/ppermute | solution.py:41
  11.0 19.9 %collective-permute-start = (bf16[2,176,1024]{2,1,0:T(8,128)(2,1)S(1)}, bf16[2,176,1024]{2,1,0:T(8,128)(2,1)}, u32[]{:S(2)}, u32[]{:S(2)}) collective-permute-start(bf16[2,176,1024]{2,1,0:T(8,128)(2,1)S(1)} %get-tuple-element.106), channel_id=1, source_target_pairs={{0,8},{8,16},{16,24},{24,32},{32,40},{40,48},{48,56},{56,64},{64,7... | collective-permute-start | bytes 2162696 | tf_op jit(solution)/shard_map/ppermute | solution.py:39
  56.5 12.0 %copy-start.1 = (bf16[1,176,3072]{2,1,0:T(8,128)(2,1)S(1)}, bf16[1,176,3072]{2,1,0:T(8,128)(2,1)}, u32[]{:S(2)}) copy-start(bf16[1,176,3072]{2,1,0:T(8,128)(2,1)} %get-tuple-element.153) | copy-start | bytes 3244036 | tf_op jit(solution)/shard_map/while
  103.6 12.0 %copy-start.1 = (bf16[1,176,3072]{2,1,0:T(8,128)(2,1)S(1)}, bf16[1,176,3072]{2,1,0:T(8,128)(2,1)}, u32[]{:S(2)}) copy-start(bf16[1,176,3072]{2,1,0:T(8,128)(2,1)} %get-tuple-element.153) | copy-start | bytes 3244036 | tf_op jit(solution)/shard_map/while
  136.5 73.0 %copy-start.6 = (bf16[176,2048]{1,0:T(8,128)(2,1)S(1)}, bf16[176,2048]{1,0:T(8,128)(2,1)}, u32[]{:S(2)}) copy-start(bf16[176,2048]{1,0:T(8,128)(2,1)} %param.10) | copy-start | bytes 2162692
  136.5 290.0 %all-gather.3.cloned.1.call-start = ((), (), s32[]{:S(2)}) async-start(), calls=%async_computation.2 | async-start | bytes 3063808 | tf_op jit(solution)/shard_map/all_gather | solution.py:127
  211.1 51.0 %copy-start.2 = (bf16[176,2048]{1,0:T(8,128)(2,1)}, bf16[176,2048]{1,0:T(8,128)(2,1)S(1)}, u32[]{:S(2)}) copy-start(bf16[176,2048]{1,0:T(8,128)(2,1)S(1)} %add_convert_fusion) | copy-start | bytes 2162692
  211.1 11.9 %collective-permute-start.2 = (bf16[176,2048]{1,0:T(8,128)(2,1)S(1)}, bf16[176,2048]{1,0:T(8,128)(2,1)S(1)}, u32[]{:S(2)}, u32[]{:S(2)}) collective-permute-start(bf16[176,2048]{1,0:T(8,128)(2,1)S(1)} %add_convert_fusion), channel_id=1, source_target_pairs={{0,1},{1,2},{2,3},{3,4},{4,5},{5,6},{6,7},{7,0},{8,9},{9,10},{10,1... | collective-permute-start | bytes 2162696 | tf_op jit(solution)/shard_map/ppermute | solution.py:19
  211.1 11.9 %collective-permute-start.3 = (bf16[176,2048]{1,0:T(8,128)(2,1)S(1)}, bf16[176,2048]{1,0:T(8,128)(2,1)S(1)}, u32[]{:S(2)}, u32[]{:S(2)}) collective-permute-start(bf16[176,2048]{1,0:T(8,128)(2,1)S(1)} %add_convert_fusion), channel_id=1, source_target_pairs={{0,7},{1,0},{2,1},{3,2},{4,3},{5,4},{6,5},{7,6},{8,15},{9,8},{10,9... | collective-permute-start | bytes 2162696 | tf_op jit(solution)/shard_map/ppermute | solution.py:24
  223.0 3.0 copy-start.5
  223.0 11.9 %collective-permute-start.4 = (bf16[176,2048]{1,0:T(8,128)(2,1)S(1)}, bf16[176,2048]{1,0:T(8,128)(2,1)S(1)}, u32[]{:S(2)}, u32[]{:S(2)}) collective-permute-start(bf16[176,2048]{1,0:T(8,128)(2,1)S(1)} %collective-permute-done.2), channel_id=1, source_target_pairs={{0,1},{1,2},{2,3},{3,4},{4,5},{5,6},{6,7},{7,0},{8,9},{9,10},{10,1... | collective-permute-start | bytes 2162696 | tf_op jit(solution)/shard_map/ppermute | solution.py:19
  223.0 23.8 %copy-start.3 = (bf16[176,2048]{1,0:T(8,128)(2,1)}, bf16[176,2048]{1,0:T(8,128)(2,1)S(1)}, u32[]{:S(2)}) copy-start(bf16[176,2048]{1,0:T(8,128)(2,1)S(1)} %collective-permute-done.3) | copy-start | bytes 2162692
  223.0 11.9 %collective-permute-start.5 = (bf16[176,2048]{1,0:T(8,128)(2,1)S(1)}, bf16[176,2048]{1,0:T(8,128)(2,1)S(1)}, u32[]{:S(2)}, u32[]{:S(2)}) collective-permute-start(bf16[176,2048]{1,0:T(8,128)(2,1)S(1)} %collective-permute-done.3), channel_id=1, source_target_pairs={{0,7},{1,0},{2,1},{3,2},{4,3},{5,4},{6,5},{7,6},{8,15},{9,8},{10,9... | collective-permute-start | bytes 2162696 | tf_op jit(solution)/shard_map/ppermute | solution.py:24
  235.0 11.9 %copy-start.4 = (bf16[176,2048]{1,0:T(8,128)(2,1)}, bf16[176,2048]{1,0:T(8,128)(2,1)S(1)}, u32[]{:S(2)}) copy-start(bf16[176,2048]{1,0:T(8,128)(2,1)S(1)} %collective-permute-done.4) | copy-start | bytes 2162692
  235.0 11.9 %collective-permute-start.6 = (bf16[176,2048]{1,0:T(8,128)(2,1)S(1)}, bf16[176,2048]{1,0:T(8,128)(2,1)S(1)}, u32[]{:S(2)}, u32[]{:S(2)}) collective-permute-start(bf16[176,2048]{1,0:T(8,128)(2,1)S(1)} %collective-permute-done.4), channel_id=1, source_target_pairs={{0,1},{1,2},{2,3},{3,4},{4,5},{5,6},{6,7},{7,0},{8,9},{9,10},{10,1... | collective-permute-start | bytes 2162696 | tf_op jit(solution)/shard_map/ppermute | solution.py:19
  235.0 87.2 %collective-permute-start.7 = (bf16[176,2048]{1,0:T(8,128)(2,1)S(1)}, bf16[176,2048]{1,0:T(8,128)(2,1)}, u32[]{:S(2)}, u32[]{:S(2)}) collective-permute-start(bf16[176,2048]{1,0:T(8,128)(2,1)S(1)} %collective-permute-done.5), channel_id=1, source_target_pairs={{0,7},{1,0},{2,1},{3,2},{4,3},{5,4},{6,5},{7,6},{8,15},{9,8},{10,9... | collective-permute-start | bytes 2162696 | tf_op jit(solution)/shard_map/ppermute | solution.py:24
  246.9 88.1 %collective-permute-start.8 = (bf16[176,2048]{1,0:T(8,128)(2,1)S(1)}, bf16[176,2048]{1,0:T(8,128)(2,1)}, u32[]{:S(2)}, u32[]{:S(2)}) collective-permute-start(bf16[176,2048]{1,0:T(8,128)(2,1)S(1)} %collective-permute-done.6), channel_id=1, source_target_pairs={{0,1},{1,2},{2,3},{3,4},{4,5},{5,6},{6,7},{7,0},{8,9},{9,10},{10,1... | collective-permute-start | bytes 2162696 | tf_op jit(solution)/shard_map/ppermute | solution.py:19
  347.8 4.3 copy-start
  347.8 6.0 %copy-start.7 = (f32[1408]{0:T(1024)S(1)}, f32[1408]{0:T(1024)}, u32[]{:S(2)}) copy-start(f32[1408]{0:T(1024)} %param.13) | copy-start | bytes 16900
  357.8 10.6 %copy-start.10 = (bf16[176,5632]{1,0:T(8,128)(2,1)S(1)}, bf16[176,5632]{1,0:T(8,128)(2,1)}, u32[]{:S(2)}) copy-start(bf16[176,5632]{1,0:T(8,128)(2,1)} %param.12) | copy-start | bytes 5947396
  368.4 5.4 %copy-start.8 = (s32[512]{0:T(512)S(1)}, s32[512]{0:T(512)}, u32[]{:S(2)}) copy-start(s32[512]{0:T(512)} %param.15) | copy-start | bytes 6148
Sparse Core Ops, SparseCore 0:
  136.7 72.8 reduce-scatter.1
  374.0 52.5 all-gather.2
